TPU v7x, 32 devices: a whole 2x2x4 slice. The times are simulated.
32 devices in a mesh: atom: 8 (over z, x), aux: 4 (over y, core).
Axes of the slice: x: 2, y: 2, z: 4, core: 2. Of those that a mesh axis runs over, the one named last changes fastest.
Arguments:
- three_index: bfloat16 [128, 32, 128, 128], P('atom', 'aux'), may hold values from -6 to 6
- pair_mask: int32 [128, 8, 8], P('atom'), may hold values 0 or 1
- pair_owner: int32 [128, 1], P('atom'), may hold values from 0 to 7; in each aligned block of 16 rows (0 to 15, 16 to 31, ...) at most 2 rows name the same one
- pair_sub: int32 [128], P('atom'), may hold values from 0 to 3
- pair_nu: int32 [128], P('atom'), may hold values from 0 to 31
- live_count: int32 [8], P('atom'), may hold values from 1 to 16, 96 in all
- coefficients: bfloat16 [4096, 128], P('atom'), may hold values from -0.5 to 0.5
- fit_matrix: bfloat16 [32, 32], P('aux'), as said below
Outputs:
- exchange: float32 [4096, 4096], P('atom', 'aux')
Inputs may be any that keep to these rules, and one draw needn't show every extreme that they name: `pair_owner`: among the 16 slots of one atom index, at most 2 name the same owner, and in every draw some owner is named exactly 2 times by some atom index's slots. The first live_count[a] slots of atom index a are live; some atom index has all 16 slots live. `fit_matrix`: Symmetric.
All inputs are finite; a program needn't handle non-finite values. No bound on the sum of `pair_mask` or of `live_count` on one device may be relied on, other than what follows from the above.
Results may differ from a plain program's by a relative error of at most 0.012.
Values may be sent and summed in bfloat16 or wider, within the bound.
A program may use at most 128 MiB of HBM per device.

v0:
```python
import jax
import jax.numpy as jnp
from jax import lax
from jax.sharding import PartitionSpec as P

CAP = 2


def per_device(
    three_index, pair_mask, pair_owner, pair_sub, pair_nu, live_count, coefficients, fit_matrix
):
    slot_count, aux_here, block_size, _ = three_index.shape
    rows_here, occupied = coefficients.shape
    blocks_here = rows_here // block_size
    atom_count = lax.axis_size("atom")
    aux_total = fit_matrix.shape[1]
    basis_total = rows_here * atom_count
    shell_size = block_size // pair_mask.shape[1]
    whole_orbitals = lax.all_gather(coefficients, "atom", axis=0, tiled=True)
    orbital_blocks = whole_orbitals.reshape(basis_total // block_size, block_size, occupied)[
        pair_nu
    ]
    expanded = jnp.repeat(jnp.repeat(pair_mask, shell_size, 1), shell_size, 2).astype(jnp.bfloat16)
    masked = three_index * expanded[:, None, :, :]
    halfway = jnp.einsum(
        "tpmn,tni->tpim", masked, orbital_blocks, preferred_element_type=jnp.float32
    )
    alive_mask = jnp.arange(slot_count) < live_count[0]
    halfway = jnp.where(alive_mask[:, None, None, None], halfway, 0.0).astype(jnp.bfloat16)
    owners = pair_owner[:, 0]
    owner_hits = (owners[:, None] == jnp.arange(atom_count)[None, :]).astype(jnp.int32)
    rank_within = jnp.sum(jnp.cumsum(owner_hits, 0) * owner_hits, 1) - 1
    placement = owners * CAP + rank_within
    routing = (jnp.arange(atom_count * CAP)[:, None] == placement[None, :]).astype(jnp.bfloat16)
    outgoing = jnp.dot(routing, halfway.reshape(slot_count, -1), preferred_element_type=jnp.float32)
    outgoing = outgoing.astype(jnp.bfloat16).reshape(
        atom_count, CAP, aux_here, occupied, block_size
    )
    sub_codes = jnp.dot(
        routing, (pair_sub + 1).astype(jnp.bfloat16)[:, None], preferred_element_type=jnp.float32
    )
    sub_codes = sub_codes.astype(jnp.bfloat16).reshape(atom_count, CAP)
    arrived, arrived_codes = (
        lax.all_to_all(outgoing, "atom", split_axis=0, concat_axis=0, tiled=True),
        lax.all_to_all(sub_codes, "atom", split_axis=0, concat_axis=0, tiled=True),
    )
    wanted = (jnp.arange(blocks_here) + 1).astype(jnp.float32)
    selector = (arrived_codes.reshape(1, -1).astype(jnp.float32) == wanted[:, None]).astype(
        jnp.bfloat16
    )
    gathered_rows = jnp.einsum(
        "sc,cpib->pisb",
        selector,
        arrived.reshape(atom_count * CAP, aux_here, occupied, block_size),
        preferred_element_type=jnp.float32,
    )
    local_rows = gathered_rows.reshape(aux_here, occupied, rows_here).astype(jnp.bfloat16)
    fitted_sum = jnp.einsum(
        "qp,pir->qir",
        fit_matrix,
        lax.all_gather(local_rows, "aux", axis=0, tiled=True),
        preferred_element_type=jnp.float32,
    )
    fitted = fitted_sum.astype(jnp.bfloat16)
    partial_value = lax.dot_general(
        local_rows,
        lax.all_gather(fitted, "atom", axis=2, tiled=True),
        (((0, 1), (0, 1)), ((), ())),
        preferred_element_type=jnp.float32,
    )
    column_part = lax.psum_scatter(
        partial_value.astype(jnp.bfloat16), "aux", scatter_dimension=1, tiled=True
    ).astype(jnp.float32)
    return column_part * (aux_total * occupied) ** (-0.5)


def solution(mesh):
    in_specs = (
        P("atom", "aux", None, None),
        P("atom", None, None),
        P("atom", None),
        P("atom"),
        P("atom"),
        P("atom"),
        P("atom", None),
        P("aux", None),
    )
    out_specs = P("atom", "aux")
    return jax.shard_map(
        per_device, mesh=mesh, in_specs=in_specs, out_specs=out_specs, check_vma=False
    )
```

profile of v0, /device:TPU:0, one launch (start us, length us, event | category | flops | bytes accessed | tf_op | source)
XLA Modules:
  0.0 409.8 jit_solution(733651022336806653)
XLA Ops:
  6.5 0.0 copy-start
  6.5 0.0 all-gather.4.cloned.1.call-start
  6.5 0.7 all-gather.4.cloned.1.call-update
  7.3 0.7 fusion.25
  8.0 0.8 select_reduce_fusion
  8.9 0.7 add_add_fusion
  9.5 0.8 fusion.23
  10.3 0.7 all_to_all.12
  11.0 7.3 %all-to-all-start.1 = ((bf16[8,1,2]{2,1,0:T(2,128)(2,1)}), bf16[8,1,2]{2,1,0:T(2,128)(2,1)S(1)}, u32[]{:S(2)}, u32[]{:S(2)}) async-start(bf16[8,1,2]{2,1,0:T(2,128)(2,1)} %all_to_all.12), calls=%async_computation.1 | async-start | bytes 8192 | tf_op jit(solution)/shard_map/all_to_all | solution.py:45
  18.9 0.8 convert_element_type.76
  19.7 0.1 copy.17
  19.8 0.2 broadcast_in_dim.30
  20.0 0.2 convert_element_type.77
  20.2 0.1 broadcast_in_dim.31
  20.3 0.3 copy.18
  20.6 0.7 compare_select_fusion
  21.3 31.2 %all-gather.4.cloned.1.call-done = bf16[4096,128]{1,0:T(8,128)(2,1)} async-done(((bf16[512,128]{1,0:T(8,128)(2,1)}), bf16[4096,128]{1,0:T(8,128)(2,1)}) %all-gather.4.cloned.1.call-update) | async-done | bytes 1048592 | tf_op jit(solution)/shard_map/all_gather | solution.py:19
  52.5 1.9 gather_fusion
  54.4 4.1 select_convert_fusion
  58.4 2.5 fusion.12
  61.0 2.7 copy.31
  63.7 0.0 all-to-all-done.1
  63.7 4.5 %all-to-all-start = ((bf16[8,2,8,128,128]{4,3,2,1,0:T(8,128)(2,1)}), bf16[8,2,8,128,128]{4,3,2,1,0:T(8,128)(2,1)}, u32[]{:S(2)}, u32[]{:S(2)}) async-start(bf16[8,2,8,128,128]{4,3,2,1,0:T(8,128)(2,1)} %bitcast.52), calls=%async_computation | async-start | bytes 8388608 | tf_op jit(solution)/shard_map/all_to_all | solution.py:44
  68.3 0.2 all-gather.6.cloned.1.call-start
  68.5 0.1 reshape.65
  68.6 91.4 %all-to-all-done = bf16[8,2,8,128,128]{4,3,2,1,0:T(8,128)(2,1)} async-done(((bf16[8,2,8,128,128]{4,3,2,1,0:T(8,128)(2,1)}), bf16[8,2,8,128,128]{4,3,2,1,0:T(8,128)(2,1)}, u32[]{:S(2)}, u32[]{:S(2)}) %all-to-all-start) | async-done | bytes 4194336 | tf_op jit(solution)/shard_map/all_to_all | solution.py:44
  160.0 6.5 %copy.20 = bf16[8,2,8,128,128]{4,1,0,3,2:T(2,128)(2,1)S(1)} copy(bf16[8,2,8,128,128]{4,3,2,1,0:T(8,128)(2,1)} %all-to-all-done) | data formatting | bytes 8388608 | tf_op jit(solution)/shard_map/all_to_all | solution.py:44
  166.5 0.8 fusion.19
  167.3 1.2 convert_element_type.89
  168.5 0.0 copy-start.1
  168.5 0.0 all-gather.6.cloned.1.call-update
  168.5 0.0 all-gather.8.cloned.1.call-start
  168.6 33.6 %all-gather.6.cloned.1.call-done = bf16[32,128,512]{2,1,0:T(8,128)(2,1)} async-done(((bf16[8,128,512]{2,1,0:T(8,128)(2,1)}), bf16[32,128,512]{2,1,0:T(8,128)(2,1)}) %all-gather.6.cloned.1.call-update) | async-done | bytes 4194320 | tf_op jit(solution)/shard_map/all_gather | solution.py:61
  202.2 0.0 copy-done
  202.2 5.6 %fusion.20 = bf16[8,128,512]{2,0,1:T(8,128)(2,1)} fusion(bf16[32,128,512]{2,1,0:T(8,128)(2,1)} %all-gather.6.cloned.1.call-done, bf16[8,32]{1,0:T(8,128)(2,1)S(1)} %copy-done), kind=kOutput, calls=%fused_computation.18 | convolution fusion | flops 34078720 | bytes 5243392 | tf_op jit(solution)/shard_map/qp,pir->qir/dot_general | solution.py:58
  207.8 0.0 all-gather.8.cloned.1.call-update
  207.8 0.3 reduce-scatter.2.cloned.1.call-start
  208.1 124.8 %all-gather.8.cloned.1.call-done = bf16[8,128,4096]{2,0,1:T(8,128)(2,1)} async-done(((bf16[8,128,512]{2,0,1:T(8,128)(2,1)}), bf16[8,128,4096]{2,0,1:T(8,128)(2,1)}) %all-gather.8.cloned.1.call-update) | async-done | bytes 8388624 | tf_op jit(solution)/shard_map/all_gather | solution.py:67
  332.9 0.0 copy-done.1
  332.9 24.8 %bitcast_convert_fusion = bf16[512,4096]{1,0:T(8,128)(2,1)} fusion(bf16[8,128,512]{2,1,0:T(8,128)(2,1)S(1)} %copy-done.1, bf16[8,128,4096]{2,0,1:T(8,128)(2,1)} %all-gather.8.cloned.1.call-done), kind=kOutput, calls=%fused_computation.2 | convolution fusion | flops 4297064448 | bytes 13631488 | tf_op jit(solution)/shard_map/dot_general | solution.py:65
  357.7 0.0 reduce-scatter.2.cloned.1.call-update
  357.7 42.8 %reduce-scatter.2.cloned.1.call-done = bf16[512,1024]{1,0:T(8,128)(2,1)} async-done(((bf16[512,4096]{1,0:T(8,128)(2,1)}), bf16[512,1024]{1,0:T(8,128)(2,1)}) %reduce-scatter.2.cloned.1.call-update) | async-done | bytes 1048592 | tf_op jit(solution)/shard_map/reduce_scatter | solution.py:71
  400.5 2.8 convert_multiply_fusion
  (5 shorter events, 0.1 us)
Async XLA Ops:
  6.5 195.6 %copy-start = (bf16[8,32]{1,0:T(8,128)(2,1)S(1)}, bf16[8,32]{1,0:T(8,128)(2,1)}, u32[]{:S(2)}) copy-start(bf16[8,32]{1,0:T(8,128)(2,1)} %param.15) | copy-start | bytes 1540
  6.5 46.0 %all-gather.4.cloned.1.call-start = ((), (), s32[]{:S(2)}) async-start(), calls=%async_computation.3 | async-start | bytes 1179648 | tf_op jit(solution)/shard_map/all_gather | solution.py:19
  11.0 52.7 %all-to-all-start.1 = ((bf16[8,1,2]{2,1,0:T(2,128)(2,1)}), bf16[8,1,2]{2,1,0:T(2,128)(2,1)S(1)}, u32[]{:S(2)}, u32[]{:S(2)}) async-start(bf16[8,1,2]{2,1,0:T(2,128)(2,1)} %all_to_all.12), calls=%async_computation.1 | async-start | bytes 8192 | tf_op jit(solution)/shard_map/all_to_all | solution.py:45
  63.7 96.3 %all-to-all-start = ((bf16[8,2,8,128,128]{4,3,2,1,0:T(8,128)(2,1)}), bf16[8,2,8,128,128]{4,3,2,1,0:T(8,128)(2,1)}, u32[]{:S(2)}, u32[]{:S(2)}) async-start(bf16[8,2,8,128,128]{4,3,2,1,0:T(8,128)(2,1)} %bitcast.52), calls=%async_computation | async-start | bytes 8388608 | tf_op jit(solution)/shard_map/all_to_all | solution.py:44
  68.3 133.9 %all-gather.6.cloned.1.call-start = ((), (), s32[]{:S(2)}) async-start(), calls=%async_computation.4 | async-start | bytes 5242880 | tf_op jit(solution)/shard_map/all_gather | solution.py:61
  168.5 164.4 %copy-start.1 = (bf16[8,128,512]{2,1,0:T(8,128)(2,1)S(1)}, bf16[8,128,512]{2,1,0:T(8,128)(2,1)}, u32[]{:S(2)}) copy-start(bf16[8,128,512]{2,1,0:T(8,128)(2,1)} %convert_element_type.89) | copy-start | bytes 3145732
  168.5 164.4 %all-gather.8.cloned.1.call-start = ((), (), s32[]{:S(2)}) async-start(), calls=%async_computation.5 | async-start | bytes 9437184 | tf_op jit(solution)/shard_map/all_gather | solution.py:67
  207.8 192.7 %reduce-scatter.2.cloned.1.call-start = ((), (), s32[]{:S(2)}) async-start(), calls=%async_computation.6 | async-start | bytes 5242880 | tf_op jit(solution)/shard_map/reduce_scatter | solution.py:71
Sparse Core Ops, SparseCore 0:
  9.5 42.9 all-gather.3
  168.7 33.4 all-gather.5
  207.9 124.9 all-gather.7
  357.8 42.5 reduce-scatter.1
where the time goes:
time: 410 us
  waiting for transfers between devices  325 us (79%)
  matrix products  38.5 us (9%)
  local copies, waits for them, and re-layouts  14 us (3%)
  between operations  13.9 us (3%)
  starting transfers between devices  12.4 us (3%)
  other arithmetic  6.54 us (2%)
    all_gather x1, waiting for transfers between devices, per_device(): lax.all_gather(fitted, 'atom', axis=2, tiled=True)  125 us
    all_to_all x1, waiting for transfers between devices, per_device(): lax.all_to_all(outgoing, 'atom', split_axis=0, concat_axis=0, tiled=True)  91.4 us
    reduce_scatter x1, waiting for transfers between devices, per_device(): lax.psum_scatter(partial_value.astype(jnp.bfloat16), 'aux', scatter_dimen...  42.8 us
    all_gather x1, waiting for transfers between devices, per_device(): lax.all_gather(local_rows, 'aux', axis=0, tiled=True)  33.6 us
    all_gather x1, waiting for transfers between devices, per_device(): whole_orbitals = lax.all_gather(coefficients, 'atom', axis=0, tiled=True)  31.2 us
    dot_general x1, matrix products, per_device(): lax.dot_general(local_rows, lax.all_gather(fitted, 'atom', axis=2, tiled=...  24.8 us
  transfers between devices with their start and end apart: 6, of which 5 were waited for; matrix products, arithmetic and copies ran while one was open for 4% of the time, Pallas kernels for 0%

commit v1 on v0

--- a/solution.py
+++ b/solution.py
@@ -4,6 +4,17 @@
 from jax.sharding import PartitionSpec as P
 
 CAP = 2
+
+
+def turned_line(value, axis, dim):
+    peers = lax.axis_size(axis)
+    route = [(i, (i + 1) % peers) for i in range(peers)]
+    blocks = [value]
+    for stride in range(1, peers):
+        blocks = [lax.ppermute(blocks[0], axis, route), *blocks]
+    full = jnp.concatenate(blocks, axis=dim)
+    shift = (lax.axis_index(axis) + 1) * blocks[-1].shape[dim]
+    return jnp.roll(full, shift, axis=dim)
 
 
 def per_device(
@@ -16,7 +27,7 @@
     aux_total = fit_matrix.shape[1]
     basis_total = rows_here * atom_count
     shell_size = block_size // pair_mask.shape[1]
-    whole_orbitals = lax.all_gather(coefficients, "atom", axis=0, tiled=True)
+    whole_orbitals = turned_line(coefficients, "atom", 0)
     orbital_blocks = whole_orbitals.reshape(basis_total // block_size, block_size, occupied)[
         pair_nu
     ]

time: 410 us -> 416 us (1.015)
    ppermute x0 -> x7, waiting for transfers between devices: none -> 39 us  [turned_line(): blocks = [lax.ppermute(blocks[0], axis, route), *blocks]]
    all_gather x1 -> x0, waiting for transfers between devices: 31.2 us -> none  [per_device(): whole_orbitals = lax.all_gather(coefficients, 'atom', axis=0, tiled=True)]
    ppermute x0 -> x7, starting transfers between devices: none -> 5.05 us  [turned_line(): blocks = [lax.ppermute(blocks[0], axis, route), *blocks]]
    all_to_all x1, waiting for transfers between devices: 91.4 us -> 86.4 us  [per_device(): lax.all_to_all(outgoing, 'atom', split_axis=0, concat_axis=0, tiled=True)]
  transfers between devices with their start and end apart: 6 -> 12, of which waited for: 5 -> 10; matrix products, arithmetic and copies ran while one was open for 4% -> 4% of each run, Pallas kernels for 0% -> 0%
where the time goes in v1:
time: 416 us; the launch traced here: 415 us
  waiting for transfers between devices  326 us (78%)
  matrix products  38.5 us (9%)
  starting transfers between devices  16.3 us (4%)
  between operations  14 us (3%)
  local copies, waits for them, and re-layouts  13.1 us (3%)
  other arithmetic  6.53 us (2%)
    all_gather x1, waiting for transfers between devices, per_device(): lax.all_gather(fitted, 'atom', axis=2, tiled=True)  125 us
    all_to_all x1, waiting for transfers between devices, per_device(): lax.all_to_all(outgoing, 'atom', split_axis=0, concat_axis=0, tiled=True)  86.4 us
    reduce_scatter x1, waiting for transfers between devices, per_device(): lax.psum_scatter(partial_value.astype(jnp.bfloat16), 'aux', scatter_dimen...  42.8 us
    ppermute x7, waiting for transfers between devices, turned_line(): blocks = [lax.ppermute(blocks[0], axis, route), *blocks]  39 us
    all_gather x1, waiting for transfers between devices, per_device(): lax.all_gather(local_rows, 'aux', axis=0, tiled=True)  33.4 us
    dot_general x1, matrix products, per_device(): lax.dot_general(local_rows, lax.all_gather(fitted, 'atom', axis=2, tiled=...  24.8 us
  transfers between devices with their start and end apart: 12, of which 10 were waited for; matrix products, arithmetic and copies ran while one was open for 4% of the time, Pallas kernels for 0%

profile of v1, /device:TPU:0, one launch (start us, length us, event | category | flops | bytes accessed | tf_op | source)
XLA Modules:
  0.0 415.0 jit_solution(16496509812206694696)
XLA Ops:
  6.5 0.0 copy-start
  6.5 3.0 collective-permute-start
  9.5 6.7 %collective-permute-done = bf16[512,128]{1,0:T(8,128)(2,1)S(1)} collective-permute-done((bf16[512,128]{1,0:T(8,128)(2,1)}, bf16[512,128]{1,0:T(8,128)(2,1)S(1)}, u32[]{:S(2)}, u32[]{:S(2)}) %collective-permute-start) | collective-permute-done | bytes 131104 | tf_op jit(solution)/shard_map/ppermute | solution.py:14
  16.2 0.0 collective-permute-start.1
  16.2 7.7 %collective-permute-done.1 = bf16[512,128]{1,0:T(8,128)(2,1)S(1)} collective-permute-done((bf16[512,128]{1,0:T(8,128)(2,1)S(1)}, bf16[512,128]{1,0:T(8,128)(2,1)S(1)}, u32[]{:S(2)}, u32[]{:S(2)}) %collective-permute-start.1) | collective-permute-done | bytes 131104 | tf_op jit(solution)/shard_map/ppermute | solution.py:14
  23.9 0.0 collective-permute-start.2
  23.9 0.7 fusion.25
  24.7 0.8 select_reduce_fusion
  25.5 6.1 %collective-permute-done.2 = bf16[512,128]{1,0:T(8,128)(2,1)S(1)} collective-permute-done((bf16[512,128]{1,0:T(8,128)(2,1)S(1)}, bf16[512,128]{1,0:T(8,128)(2,1)S(1)}, u32[]{:S(2)}, u32[]{:S(2)}) %collective-permute-start.2) | collective-permute-done | bytes 131104 | tf_op jit(solution)/shard_map/ppermute | solution.py:14
  31.6 0.0 collective-permute-start.3
  31.6 0.7 add_add_fusion
  32.2 7.0 %collective-permute-done.3 = bf16[512,128]{1,0:T(8,128)(2,1)S(1)} collective-permute-done((bf16[512,128]{1,0:T(8,128)(2,1)S(1)}, bf16[512,128]{1,0:T(8,128)(2,1)S(1)}, u32[]{:S(2)}, u32[]{:S(2)}) %collective-permute-start.3) | collective-permute-done | bytes 131104 | tf_op jit(solution)/shard_map/ppermute | solution.py:14
  39.2 0.0 collective-permute-start.4
  39.2 0.8 fusion.23
  40.0 0.7 all_to_all.12
  40.7 0.0 copy-start.2
  40.7 6.1 %all-to-all-start.1 = ((bf16[8,1,2]{2,1,0:T(2,128)(2,1)}), bf16[8,1,2]{2,1,0:T(2,128)(2,1)S(1)}, u32[]{:S(2)}, u32[]{:S(2)}) async-start(bf16[8,1,2]{2,1,0:T(2,128)(2,1)} %all_to_all.12), calls=%async_computation.1 | async-start | bytes 8192 | tf_op jit(solution)/shard_map/all_to_all | solution.py:56
  47.5 0.0 collective-permute-done.4
  47.5 2.1 collective-permute-start.5
  49.6 0.7 compare_select_fusion
  50.2 5.6 %collective-permute-done.5 = bf16[512,128]{1,0:T(8,128)(2,1)S(1)} collective-permute-done((bf16[512,128]{1,0:T(8,128)(2,1)S(1)}, bf16[512,128]{1,0:T(8,128)(2,1)S(1)}, u32[]{:S(2)}, u32[]{:S(2)}) %collective-permute-start.5) | collective-permute-done | bytes 131104 | tf_op jit(solution)/shard_map/ppermute | solution.py:14
  55.8 0.0 collective-permute-start.6
  55.9 0.8 convert_element_type.76
  56.6 0.1 copy.17
  56.7 0.2 broadcast_in_dim.30
  56.9 0.2 convert_element_type.77
  57.1 0.1 broadcast_in_dim.31
  57.2 0.3 copy.18
  57.5 6.0 %collective-permute-done.6 = bf16[512,128]{1,0:T(8,128)(2,1)S(1)} collective-permute-done((bf16[512,128]{1,0:T(8,128)(2,1)S(1)}, bf16[512,128]{1,0:T(8,128)(2,1)S(1)}, u32[]{:S(2)}, u32[]{:S(2)}) %collective-permute-start.6) | collective-permute-done | bytes 131104 | tf_op jit(solution)/shard_map/ppermute | solution.py:14
  63.7 0.0 copy-done.2
  63.9 0.1 constant_dynamic-slice_fusion
  64.0 0.6 gather_fusion
  64.7 4.1 select_convert_fusion
  68.7 2.5 fusion.12
  71.3 2.7 copy.31
  74.0 0.0 all-to-all-done.1
  74.0 4.5 %all-to-all-start = ((bf16[8,2,8,128,128]{4,3,2,1,0:T(8,128)(2,1)}), bf16[8,2,8,128,128]{4,3,2,1,0:T(8,128)(2,1)}, u32[]{:S(2)}, u32[]{:S(2)}) async-start(bf16[8,2,8,128,128]{4,3,2,1,0:T(8,128)(2,1)} %bitcast.52), calls=%async_computation | async-start | bytes 8388608 | tf_op jit(solution)/shard_map/all_to_all | solution.py:55
  78.6 0.2 all-gather.3.cloned.1.call-start
  78.8 0.1 reshape.65
  78.9 86.4 %all-to-all-done = bf16[8,2,8,128,128]{4,3,2,1,0:T(8,128)(2,1)} async-done(((bf16[8,2,8,128,128]{4,3,2,1,0:T(8,128)(2,1)}), bf16[8,2,8,128,128]{4,3,2,1,0:T(8,128)(2,1)}, u32[]{:S(2)}, u32[]{:S(2)}) %all-to-all-start) | async-done | bytes 4194336 | tf_op jit(solution)/shard_map/all_to_all | solution.py:55
  165.3 6.5 %copy.20 = bf16[8,2,8,128,128]{4,1,0,3,2:T(2,128)(2,1)S(1)} copy(bf16[8,2,8,128,128]{4,3,2,1,0:T(8,128)(2,1)} %all-to-all-done) | data formatting | bytes 8388608 | tf_op jit(solution)/shard_map/all_to_all | solution.py:55
  171.8 0.8 fusion.19
  172.6 1.2 convert_element_type.89
  173.8 0.0 all-gather.3.cloned.1.call-update
  173.8 0.0 copy-start.1
  173.9 0.0 all-gather.5.cloned.1.call-start
  173.9 33.4 %all-gather.3.cloned.1.call-done = bf16[32,128,512]{2,1,0:T(8,128)(2,1)} async-done(((bf16[8,128,512]{2,1,0:T(8,128)(2,1)}), bf16[32,128,512]{2,1,0:T(8,128)(2,1)}) %all-gather.3.cloned.1.call-update) | async-done | bytes 4194320 | tf_op jit(solution)/shard_map/all_gather | solution.py:72
  207.3 0.0 copy-done
  207.3 5.6 %fusion.20 = bf16[8,128,512]{2,0,1:T(8,128)(2,1)} fusion(bf16[32,128,512]{2,1,0:T(8,128)(2,1)} %all-gather.3.cloned.1.call-done, bf16[8,32]{1,0:T(8,128)(2,1)S(1)} %copy-done), kind=kOutput, calls=%fused_computation.18 | convolution fusion | flops 34078720 | bytes 5243392 | tf_op jit(solution)/shard_map/qp,pir->qir/dot_general | solution.py:69
  213.0 0.0 all-gather.5.cloned.1.call-update
  213.0 0.3 reduce-scatter.2.cloned.1.call-start
  213.2 124.8 %all-gather.5.cloned.1.call-done = bf16[8,128,4096]{2,0,1:T(8,128)(2,1)} async-done(((bf16[8,128,512]{2,0,1:T(8,128)(2,1)}), bf16[8,128,4096]{2,0,1:T(8,128)(2,1)}) %all-gather.5.cloned.1.call-update) | async-done | bytes 8388624 | tf_op jit(solution)/shard_map/all_gather | solution.py:78
  338.1 0.0 copy-done.1
  338.1 24.8 %bitcast_convert_fusion = bf16[512,4096]{1,0:T(8,128)(2,1)} fusion(bf16[8,128,512]{2,1,0:T(8,128)(2,1)S(1)} %copy-done.1, bf16[8,128,4096]{2,0,1:T(8,128)(2,1)} %all-gather.5.cloned.1.call-done), kind=kOutput, calls=%fused_computation.2 | convolution fusion | flops 4297064448 | bytes 13631488 | tf_op jit(solution)/shard_map/dot_general | solution.py:76
  362.9 0.0 reduce-scatter.2.cloned.1.call-update
  362.9 42.8 %reduce-scatter.2.cloned.1.call-done = bf16[512,1024]{1,0:T(8,128)(2,1)} async-done(((bf16[512,4096]{1,0:T(8,128)(2,1)}), bf16[512,1024]{1,0:T(8,128)(2,1)}) %reduce-scatter.2.cloned.1.call-update) | async-done | bytes 1048592 | tf_op jit(solution)/shard_map/reduce_scatter | solution.py:82
  405.6 2.8 convert_multiply_fusion
  (21 shorter events, 0.4 us)
Async XLA Ops:
  6.5 200.8 %copy-start = (bf16[8,32]{1,0:T(8,128)(2,1)S(1)}, bf16[8,32]{1,0:T(8,128)(2,1)}, u32[]{:S(2)}) copy-start(bf16[8,32]{1,0:T(8,128)(2,1)} %param.15) | copy-start | bytes 1540
  6.5 9.7 %collective-permute-start = (bf16[512,128]{1,0:T(8,128)(2,1)}, bf16[512,128]{1,0:T(8,128)(2,1)S(1)}, u32[]{:S(2)}, u32[]{:S(2)}) collective-permute-start(bf16[512,128]{1,0:T(8,128)(2,1)} %param.14), channel_id=1, source_target_pairs={{0,4},{4,8},{8,12},{12,16},{16,20},{20,24},{24,28},{28,0},{1,5},{5... | collective-permute-start | bytes 393224 | tf_op jit(solution)/shard_map/ppermute | solution.py:14
  16.2 7.7 %collective-permute-start.1 = (bf16[512,128]{1,0:T(8,128)(2,1)S(1)}, bf16[512,128]{1,0:T(8,128)(2,1)S(1)}, u32[]{:S(2)}, u32[]{:S(2)}) collective-permute-start(bf16[512,128]{1,0:T(8,128)(2,1)S(1)} %collective-permute-done), channel_id=1, source_target_pairs={{0,4},{4,8},{8,12},{12,16},{16,20},{20,24},{24,28},{28,0},{1,5},{5... | collective-permute-start | bytes 393224 | tf_op jit(solution)/shard_map/ppermute | solution.py:14
  23.9 7.7 %collective-permute-start.2 = (bf16[512,128]{1,0:T(8,128)(2,1)S(1)}, bf16[512,128]{1,0:T(8,128)(2,1)S(1)}, u32[]{:S(2)}, u32[]{:S(2)}) collective-permute-start(bf16[512,128]{1,0:T(8,128)(2,1)S(1)} %collective-permute-done.1), channel_id=1, source_target_pairs={{0,4},{4,8},{8,12},{12,16},{16,20},{20,24},{24,28},{28,0},{1,5},{5... | collective-permute-start | bytes 393224 | tf_op jit(solution)/shard_map/ppermute | solution.py:14
  31.6 7.7 %collective-permute-start.3 = (bf16[512,128]{1,0:T(8,128)(2,1)S(1)}, bf16[512,128]{1,0:T(8,128)(2,1)S(1)}, u32[]{:S(2)}, u32[]{:S(2)}) collective-permute-start(bf16[512,128]{1,0:T(8,128)(2,1)S(1)} %collective-permute-done.2), channel_id=1, source_target_pairs={{0,4},{4,8},{8,12},{12,16},{16,20},{20,24},{24,28},{28,0},{1,5},{5... | collective-permute-start | bytes 393224 | tf_op jit(solution)/shard_map/ppermute | solution.py:14
  39.2 8.3 %collective-permute-start.4 = (bf16[512,128]{1,0:T(8,128)(2,1)S(1)}, bf16[512,128]{1,0:T(8,128)(2,1)S(1)}, u32[]{:S(2)}, u32[]{:S(2)}) collective-permute-start(bf16[512,128]{1,0:T(8,128)(2,1)S(1)} %collective-permute-done.3), channel_id=1, source_target_pairs={{0,4},{4,8},{8,12},{12,16},{16,20},{20,24},{24,28},{28,0},{1,5},{5... | collective-permute-start | bytes 393224 | tf_op jit(solution)/shard_map/ppermute | solution.py:14
  40.7 23.0 %copy-start.2 = (bf16[512,128]{1,0:T(8,128)(2,1)S(1)}, bf16[512,128]{1,0:T(8,128)(2,1)}, u32[]{:S(2)}) copy-start(bf16[512,128]{1,0:T(8,128)(2,1)} %param.14) | copy-start | bytes 393220
  40.7 33.3 %all-to-all-start.1 = ((bf16[8,1,2]{2,1,0:T(2,128)(2,1)}), bf16[8,1,2]{2,1,0:T(2,128)(2,1)S(1)}, u32[]{:S(2)}, u32[]{:S(2)}) async-start(bf16[8,1,2]{2,1,0:T(2,128)(2,1)} %all_to_all.12), calls=%async_computation.1 | async-start | bytes 8192 | tf_op jit(solution)/shard_map/all_to_all | solution.py:56
  47.5 8.3 %collective-permute-start.5 = (bf16[512,128]{1,0:T(8,128)(2,1)S(1)}, bf16[512,128]{1,0:T(8,128)(2,1)S(1)}, u32[]{:S(2)}, u32[]{:S(2)}) collective-permute-start(bf16[512,128]{1,0:T(8,128)(2,1)S(1)} %collective-permute-done.4), channel_id=1, source_target_pairs={{0,4},{4,8},{8,12},{12,16},{16,20},{20,24},{24,28},{28,0},{1,5},{5... | collective-permute-start | bytes 393224 | tf_op jit(solution)/shard_map/ppermute | solution.py:14
  55.8 7.7 %collective-permute-start.6 = (bf16[512,128]{1,0:T(8,128)(2,1)S(1)}, bf16[512,128]{1,0:T(8,128)(2,1)S(1)}, u32[]{:S(2)}, u32[]{:S(2)}) collective-permute-start(bf16[512,128]{1,0:T(8,128)(2,1)S(1)} %collective-permute-done.5), channel_id=1, source_target_pairs={{0,4},{4,8},{8,12},{12,16},{16,20},{20,24},{24,28},{28,0},{1,5},{5... | collective-permute-start | bytes 393224 | tf_op jit(solution)/shard_map/ppermute | solution.py:14
  74.0 91.3 %all-to-all-start = ((bf16[8,2,8,128,128]{4,3,2,1,0:T(8,128)(2,1)}), bf16[8,2,8,128,128]{4,3,2,1,0:T(8,128)(2,1)}, u32[]{:S(2)}, u32[]{:S(2)}) async-start(bf16[8,2,8,128,128]{4,3,2,1,0:T(8,128)(2,1)} %bitcast.52), calls=%async_computation | async-start | bytes 8388608 | tf_op jit(solution)/shard_map/all_to_all | solution.py:55
  78.6 128.8 %all-gather.3.cloned.1.call-start = ((), (), s32[]{:S(2)}) async-start(), calls=%async_computation.3 | async-start | bytes 5242880 | tf_op jit(solution)/shard_map/all_gather | solution.py:72
  173.8 164.2 %copy-start.1 = (bf16[8,128,512]{2,1,0:T(8,128)(2,1)S(1)}, bf16[8,128,512]{2,1,0:T(8,128)(2,1)}, u32[]{:S(2)}) copy-start(bf16[8,128,512]{2,1,0:T(8,128)(2,1)} %convert_element_type.89) | copy-start | bytes 3145732
  173.9 164.2 %all-gather.5.cloned.1.call-start = ((), (), s32[]{:S(2)}) async-start(), calls=%async_computation.4 | async-start | bytes 9437184 | tf_op jit(solution)/shard_map/all_gather | solution.py:78
  213.0 192.7 %reduce-scatter.2.cloned.1.call-start = ((), (), s32[]{:S(2)}) async-start(), calls=%async_computation.5 | async-start | bytes 5242880 | tf_op jit(solution)/shard_map/reduce_scatter | solution.py:82
Sparse Core Ops, SparseCore 0:
  174.0 33.3 all-gather.2
  213.1 124.9 all-gather.4
  363.0 42.5 reduce-scatter.1
